TPU v7x, 128 devices: a whole 4x4x4 slice. The times are simulated.
128 devices in a mesh: gx: 8 (over y, core), gy: 16 (over z, x).
Axes of the slice: x: 4, y: 4, z: 4, core: 2. Of those that a mesh axis runs over, the one named last changes fastest.
Arguments:
- face_block: float32 [8, 16, 4, 512, 512], P('gx', 'gy'), may hold values from -40 to 40, as said below
- coupling: float32 [8, 16, 4, 512, 1024], P('gx', 'gy'), may hold values from -1.1 to 1.1
- interior_inverse: float32 [8, 16, 1024, 1024], P('gx', 'gy'), may hold values from -5 to 5, as said below
- face_values: float32 [8, 16, 4, 512, 128], P('gx', 'gy'), may hold values from -6 to 6
- adjacency: int32 [8, 16, 4], P('gx', 'gy'), may hold values from 0 to 1, as said below
- primal_basis: float32 [8, 16, 2048, 384], P('gx', 'gy'), may hold values from -0.125 to 0.125
- primal_matrix: float32 [8, 16, 384, 384], P('gx', 'gy'), may hold values from -0.15625 to 0.15625
- primal_map: int32 [8, 16, 384], P('gx', 'gy'), may hold values from 0 to 16383, as said below
- primal_count: int32 [8, 16], P('gx', 'gy'), may hold values from 128 to 384, as said below
Outputs:
- averaged: float32 [8, 16, 4, 512, 128], P('gx', 'gy')
- coarse_product: float32 [16384, 128], P(('gx', 'gy'))
Inputs may be any that keep to these rules, and one draw needn't show every extreme that they name: `adjacency`: equal on both sides of every face and 0 on the faces at the grid's outer boundary. `primal_map`: coarse rows (a 16 + b) * 128 to (a 16 + b + 1) * 128 - 1 form the block of the subdomain at grid position (a, b). Every row of the subdomain at (i, j) lies in the block of the subdomain at (i, j), (i - 1, j), (i, j - 1) or (i - 1, j - 1); its rows below primal_count are distinct. `primal_count`: at most 128 times the number of the blocks named for primal_map that lie inside the grid; some subdomain has exactly 384 live primal unknowns. interior_inverse is symmetric positive definite. face_block is symmetric, and face_block minus the condensed interior term is positive definite.
All inputs are finite; a program needn't handle non-finite values.
Results may differ from a plain program's by a relative error of at most 0.000062.
Values sent between devices are 32-bit elements; how exact they have to be, the bound alone decides.
A program may use at most 128 MiB of HBM per device.

v0:
```python
import jax
import jax.numpy as jnp
from jax import lax
from jax.sharding import PartitionSpec as P

CB = 128


def padded(x, sides, width):
    for axis, dim in sides:
        count, length = (lax.axis_size(axis), x.shape[dim])
        up = [(i, (i + 1) % count) for i in range(count - 1)]
        down = [(j, i) for i, j in up]
        last = lax.slice_in_dim(x, length - width, length, axis=dim)
        first = lax.slice_in_dim(x, 0, width, axis=dim)
        before = lax.ppermute(last, axis, up)
        after = lax.ppermute(first, axis, down)
        x = jnp.concatenate([before, x, after], axis=dim)
    return x


def from_behind(block, axis, distance):
    devices = range(lax.axis_size(axis))
    route = [(i - distance, i) for i in devices if i - distance in devices]
    return lax.ppermute(block, axis, route)


def condense(blocks, couple, inverse, values):
    face_count, face_size, inner_size = couple.shape
    left_part = jnp.dot(
        couple.reshape(face_count * face_size, inner_size),
        inverse,
        precision=lax.Precision.HIGHEST,
        preferred_element_type=jnp.float32,
    )
    left_part = left_part.reshape(face_count, face_size, inner_size)
    schur_block = blocks - jnp.einsum(
        "fan,fbn->fab", left_part, couple, precision=lax.Precision.HIGHEST
    )
    weighted = jnp.einsum("fab,fbr->far", schur_block, values, precision=lax.Precision.HIGHEST)
    return (schur_block, weighted)


def deluxe_solve(summed_matrix, rhs_side):
    factor = jnp.linalg.cholesky(summed_matrix)
    inner_part = lax.linalg.triangular_solve(factor, rhs_side, left_side=True, lower=True)
    return lax.linalg.triangular_solve(
        factor, inner_part, left_side=True, lower=True, transpose_a=True
    )


def contract_rows(left_mat, right_mat):
    return lax.dot_general(
        left_mat,
        right_mat,
        (((0,), (0,)), ((), ())),
        precision=lax.Precision.HIGHEST,
        preferred_element_type=jnp.float32,
    )


def shards(
    face_block,
    coupling,
    interior_inverse,
    face_values,
    adjacency,
    primal_basis,
    primal_matrix,
    primal_map,
    primal_count,
):
    schur_block, weighted = condense(
        face_block[0, 0], coupling[0, 0], interior_inverse[0, 0], face_values[0, 0]
    )
    face_size = schur_block.shape[1]
    packed = jnp.concatenate([schur_block, weighted], axis=2)
    x_side = padded(packed[0:2], (("gx", 0),), 1)
    y_side = padded(packed[2:4], (("gy", 0),), 1)
    across = jnp.stack([x_side[0], x_side[3], y_side[0], y_side[3]], axis=0)
    across = across * adjacency[0, 0].astype(jnp.float32)[:, None, None]
    summed_matrix = schur_block + across[:, :, :face_size]
    rhs_side = weighted + across[:, :, face_size:]
    averaged = deluxe_solve(summed_matrix, rhs_side)
    face_count = averaged.shape[0]
    rhs_count = averaged.shape[2]
    local_basis = primal_basis[0, 0]
    primal_size = local_basis.shape[1]
    live_mask = (jnp.arange(primal_size, dtype=jnp.int32) < primal_count[0, 0]).astype(jnp.float32)[
        :, None
    ]
    primal = (
        contract_rows(local_basis, averaged.reshape(face_count * face_size, rhs_count)) * live_mask
    )
    primal_rows = primal_map[0, 0]
    across_y = lax.axis_size("gy")
    step_x = lax.axis_index("gx") - primal_rows // (across_y * CB)
    step_y = lax.axis_index("gy") - primal_rows // CB % across_y
    window_rows = (step_x * 2 + step_y) * CB + primal_rows % CB
    window_terms = (
        jnp.zeros((4 * CB, rhs_count), jnp.float32)
        .at[window_rows]
        .add(primal)
        .reshape(2, 2, CB, rhs_count)
    )
    from_right = from_behind(window_terms[1], "gx", -1)
    column_terms = window_terms[0] + from_right
    from_above = from_behind(column_terms[1], "gy", -1)
    own_residual = column_terms[0] + from_above
    from_left = from_behind(own_residual, "gx", 1)
    pair_x = jnp.stack([own_residual, from_left], axis=0)
    from_below = from_behind(pair_x, "gy", 1)
    window_residual = jnp.stack([pair_x, from_below], axis=1).reshape(4 * CB, rhs_count)
    picked = jnp.take(window_residual, window_rows, axis=0) * live_mask
    local_terms = (
        jnp.dot(
            primal_matrix[0, 0],
            picked,
            precision=lax.Precision.HIGHEST,
            preferred_element_type=jnp.float32,
        )
        * live_mask
    )
    window_product = (
        jnp.zeros((4 * CB, rhs_count), jnp.float32)
        .at[window_rows]
        .add(local_terms)
        .reshape(2, 2, CB, rhs_count)
    )
    product_right = from_behind(window_product[1], "gx", -1)
    column_product = window_product[0] + product_right
    product_above = from_behind(column_product[1], "gy", -1)
    coarse_product = column_product[0] + product_above
    return (averaged[None, None], coarse_product)


def solution(mesh):
    in_specs = (
        P("gx", "gy", None, None, None),
        P("gx", "gy", None, None, None),
        P("gx", "gy", None, None),
        P("gx", "gy", None, None, None),
        P("gx", "gy", None),
        P("gx", "gy", None, None),
        P("gx", "gy", None, None),
        P("gx", "gy", None),
        P("gx", "gy"),
    )
    out_specs = (P("gx", "gy", None, None, None), P(("gx", "gy"), None))
    return jax.shard_map(shards, mesh=mesh, in_specs=in_specs, out_specs=out_specs, check_vma=False)
```

profile of v0, /device:TPU:1, one launch (start us, length us, event | category | flops | bytes accessed | tf_op | source)
XLA Modules:
  0.0 710.5 jit_solution(10699471028197721425)
XLA Ops:
  0.6 5.4 copy.51
  6.1 32.7 %fusion.2 = f32[4,512,1024]{2,1,0:T(8,128)} fusion(f32[1,1,4,512,1024]{4,3,2,1,0:T(8,128)} %param.10, f32[1,1,1024,1024]{3,2,1,0:T(8,128)} %param.11), kind=kOutput, calls=%fused_computation.10 | convolution fusion | flops 25769803776 | bytes 20971520 | tf_op jit(solution)/shard_map/dot_general | solution.py:30
  38.8 16.4 %bitcast_subtract_fusion = f32[4,512,512]{1,2,0:T(8,128)S(1)} fusion(f32[1,1,4,512,512]{3,4,2,1,0:T(8,128)S(1)} %copy-done.4, f32[4,512,1024]{2,1,0:T(8,128)} %fusion.2, f32[1,1,4,512,1024]{4,3,2,1,0:T(8,128)S(1)} %copy-done.8), kind=kOutput, calls=%fused_computation.20 | convolution fusion | flops 12885950464 | bytes 25165824 | tf_op jit(solution)/shard_map/fan,fbn->fab/dot_general | solution.py:37
  60.8 4.6 collective-permute-start
  68.6 5.6 collective-permute-start.2
  75.8 4.4 collective-permute-done
  80.2 4.7 collective-permute-done.1
  84.9 14.1 %collective-permute-done.3 = f32[1,512,640]{1,2,0:T(8,128)} collective-permute-done((f32[1,512,640]{1,2,0:T(8,128)}, f32[1,512,640]{1,2,0:T(8,128)}, u32[]{:S(2)}, u32[]{:S(2)}) %collective-permute-start.3) | collective-permute-done | bytes 1310752 | tf_op jit(solution)/shard_map/ppermute | solution.py:17
  100.7 3.4 maximum_multiply_fusion
  108.4 5.2 copy.54
  113.6 4.5 fusion.5
  120.8 47.7 %custom-call.36 = f32[4,128,128]{2,1,0:T(8,128)S(1)} custom-call(f32[4,128,128]{2,1,0:T(8,128)} %cholesky.274), custom_call_target="Cholesky" | custom-call | tf_op jit(solution)/shard_map/jit(cholesky)/cholesky | solution.py:45
  169.2 40.8 %custom-call.37 = f32[4,1,128,128]{2,3,1,0:T(8,128)} custom-call(f32[4,1,128,128]{3,2,1,0:T(8,128)} %select_bitcast_fusion.2), custom_call_target="InvertDiagBlocksLowerTriangular" | custom-call | tf_op jit(solution)/shard_map/jit(cholesky)/cholesky | solution.py:45
  212.5 3.0 constant_dynamic-update-slice_fusion.3
  219.0 48.5 %custom-call.38 = f32[4,128,128]{2,1,0:T(8,128)} custom-call(f32[4,128,128]{2,1,0:T(8,128)} %cholesky.278), custom_call_target="Cholesky" | custom-call | tf_op jit(solution)/shard_map/jit(cholesky)/cholesky | solution.py:45
  269.3 40.7 %custom-call.39 = f32[4,1,128,128]{2,3,1,0:T(8,128)} custom-call(f32[4,1,128,128]{3,2,1,0:T(8,128)} %get-tuple-element.37), custom_call_target="InvertDiagBlocksLowerTriangular" | custom-call | tf_op jit(solution)/shard_map/jit(cholesky)/cholesky | solution.py:45
  316.9 48.3 %custom-call.40 = f32[4,128,128]{2,1,0:T(8,128)} custom-call(f32[4,128,128]{2,1,0:T(8,128)} %cholesky.283), custom_call_target="Cholesky" | custom-call | tf_op jit(solution)/shard_map/jit(cholesky)/cholesky | solution.py:45
  367.1 40.9 %custom-call.41 = f32[4,1,128,128]{2,3,1,0:T(8,128)} custom-call(f32[4,1,128,128]{3,2,1,0:T(8,128)} %get-tuple-element.35), custom_call_target="InvertDiagBlocksLowerTriangular" | custom-call | tf_op jit(solution)/shard_map/jit(cholesky)/cholesky | solution.py:45
  410.2 3.4 slice_subtract_fusion.8
  413.5 48.4 %custom-call.42 = f32[4,128,128]{2,1,0:T(8,128)} custom-call(f32[4,128,128]{2,1,0:T(8,128)} %slice_subtract_fusion.8), custom_call_target="Cholesky" | custom-call | tf_op jit(solution)/shard_map/jit(cholesky)/cholesky | solution.py:45
  464.2 5.0 select_select_fusion
  469.1 15.3 %while.1 = (s32[]{:T(128)}, f32[4,512,512]{2,1,0:T(8,128)}, s32[4,2]{0,1:T(2,128)S(1)}, f32[4,4,128,128]{3,2,0,1:T(8,128)}, s32[]{:T(128)}) while((s32[]{:T(128)}, f32[4,512,512]{2,1,0:T(8,128)}, s32[4,2]{0,1:T(2,128)S(1)}, f32[4,4,128,128]{3,2,0,1:T(8,128)}, s32[]{:T(128)}) %tuple.40), condition=%wide.while_cond, body=%wide.while_body.sunk | while | flops 2 | bytes 525421 | solution.py:47
  469.8 3.2 bitcast_dynamic-update-slice_fusion.2
  473.6 3.2 bitcast_dynamic-update-slice_fusion.2
  477.5 3.2 bitcast_dynamic-update-slice_fusion.2
  481.3 3.1 bitcast_dynamic-update-slice_fusion.2
  484.4 159.0 %custom-call.43 = f32[4,4,128,128]{2,3,1,0:T(8,128)} custom-call(f32[4,4,128,128]{3,2,1,0:T(8,128)} %bitcast.153), custom_call_target="InvertDiagBlocksLowerTriangular" | custom-call | tf_op jit(solution)/shard_map/triangular_solve | solution.py:47
  668.8 4.9 collective-permute-done.4
  675.0 4.4 collective-permute-done.5
  683.5 3.8 collective-permute-start.7
  698.8 5.1 collective-permute-done.8
  705.2 4.4 collective-permute-done.9
  (113 shorter events, 86.5 us)
Async XLA Ops:
  0.6 660.4 %copy-start = (f32[1,1,2048,384]{3,2,1,0:T(8,128)S(1)}, f32[1,1,2048,384]{3,2,1,0:T(8,128)}, u32[]{:S(2)}) copy-start(f32[1,1,2048,384]{3,2,1,0:T(8,128)} %param.14) | copy-start | bytes 9437188
  6.0 32.7 %copy-start.4 = (f32[1,1,4,512,512]{3,4,2,1,0:T(8,128)S(1)}, f32[1,1,4,512,512]{3,4,2,1,0:T(8,128)}, u32[]{:S(2)}) copy-start(f32[1,1,4,512,512]{3,4,2,1,0:T(8,128)} %copy.51) | copy-start | bytes 12582916
  6.0 32.7 %copy-start.8 = (f32[1,1,4,512,1024]{4,3,2,1,0:T(8,128)S(1)}, f32[1,1,4,512,1024]{4,3,2,1,0:T(8,128)}, u32[]{:S(2)}) copy-start(f32[1,1,4,512,1024]{4,3,2,1,0:T(8,128)} %param.10) | copy-start | bytes 25165828
  38.8 16.4 %copy-start.12 = (f32[1,1,4,512,128]{4,3,2,1,0:T(8,128)S(1)}, f32[1,1,4,512,128]{4,3,2,1,0:T(8,128)}, u32[]{:S(2)}) copy-start(f32[1,1,4,512,128]{4,3,2,1,0:T(8,128)} %param.12) | copy-start | bytes 3145732
  55.2 5.6 copy-start.1
  58.1 2.7 copy-start.6
  58.1 16.7 %copy-start.14 = (s32[1,1,384]{2,1,0:T(1,128)S(1)}, s32[1,1,384]{2,1,0:T(1,128)}, u32[]{:S(2)}) copy-start(s32[1,1,384]{2,1,0:T(1,128)} %param.16) | copy-start | bytes 4612
  58.1 17.6 %copy-start.15 = (s32[1,1,4]{2,1,0:T(1,128)S(1)}, s32[1,1,4]{2,1,0:T(1,128)}, u32[]{:S(2)}) copy-start(s32[1,1,4]{2,1,0:T(1,128)} %param.13) | copy-start | bytes 52
  60.8 19.4 %collective-permute-start = (f32[1,512,640]{1,2,0:T(8,128)}, f32[1,512,640]{1,2,0:T(8,128)}, u32[]{:S(2)}, u32[]{:S(2)}) collective-permute-start(f32[1,512,640]{1,2,0:T(8,128)} %get-tuple-element.24), channel_id=1, source_target_pairs={{0,16},{16,32},{32,48},{48,64},{64,80},{80,96},{96,112},{1,17},{17... | collective-permute-start | bytes 3932168 | tf_op jit(solution)/shard_map/ppermute | solution.py:16
  65.4 19.5 %collective-permute-start.1 = (f32[1,512,640]{1,2,0:T(8,128)}, f32[1,512,640]{1,2,0:T(8,128)}, u32[]{:S(2)}, u32[]{:S(2)}) collective-permute-start(f32[1,512,640]{1,2,0:T(8,128)} %get-tuple-element.25), channel_id=1, source_target_pairs={{16,0},{32,16},{48,32},{64,48},{80,64},{96,80},{112,96},{17,1},{33... | collective-permute-start | bytes 3932168 | tf_op jit(solution)/shard_map/ppermute | solution.py:17
  67.3 31.7 %collective-permute-start.3 = (f32[1,512,640]{1,2,0:T(8,128)}, f32[1,512,640]{1,2,0:T(8,128)}, u32[]{:S(2)}, u32[]{:S(2)}) collective-permute-start(f32[1,512,640]{1,2,0:T(8,128)} %get-tuple-element.26), channel_id=1, source_target_pairs={{1,0},{2,1},{3,2},{4,3},{5,4},{6,5},{7,6},{8,7},{9,8},{10,9},{11,1... | collective-permute-start | bytes 3932168 | tf_op jit(solution)/shard_map/ppermute | solution.py:17
  68.6 32.2 %collective-permute-start.2 = (f32[1,512,640]{1,2,0:T(8,128)}, f32[1,512,640]{1,2,0:T(8,128)}, u32[]{:S(2)}, u32[]{:S(2)}) collective-permute-start(f32[1,512,640]{1,2,0:T(8,128)} %get-tuple-element.27), channel_id=1, source_target_pairs={{0,1},{1,2},{2,3},{3,4},{4,5},{5,6},{6,7},{7,8},{8,9},{9,10},{10,1... | collective-permute-start | bytes 3932168 | tf_op jit(solution)/shard_map/ppermute | solution.py:16
  75.8 28.4 %copy-start.7 = (f32[4,512,128]{1,2,0:T(8,128)S(1)}, f32[4,512,128]{1,2,0:T(8,128)}, u32[]{:S(2)}) copy-start(f32[4,512,128]{1,2,0:T(8,128)} %copy-done.6) | copy-start | bytes 3145732
  100.7 4.7 copy-start.2
  118.1 1.9 copy-start.5
  210.0 2.5 copy-start.13
  217.4 0.9 copy-start.10
  315.4 0.8 copy-start.11
  643.5 8.7 %copy-start.3 = (f32[4,512,512]{2,1,0:T(8,128)S(1)}, f32[4,512,512]{2,1,0:T(8,128)}, u32[]{:S(2)}) copy-start(f32[4,512,512]{2,1,0:T(8,128)} %get-tuple-element.93) | copy-start | bytes 12582916
  643.5 10.2 %copy-start.9 = (f32[4,4,128,128]{2,3,1,0:T(8,128)S(1)}, f32[4,4,128,128]{2,3,1,0:T(8,128)}, u32[]{:S(2)}) copy-start(f32[4,4,128,128]{2,3,1,0:T(8,128)} %custom-call.43) | copy-start | bytes 3145732
  666.8 6.9 collective-permute-start.4
  673.7 5.7 collective-permute-start.5
  679.5 4.0 collective-permute-start.6
  683.5 6.5 collective-permute-start.7
  696.9 7.0 collective-permute-start.8
  703.9 5.7 collective-permute-start.9
where the time goes:
time: 723 us; the launch traced here: 710 us
  other arithmetic  508 us (70%)
  matrix products  88.9 us (12%)
  waiting for transfers between devices  47.8 us (7%)
  local copies, waits for them, and re-layouts  37.6 us (5%)
  starting transfers between devices  26.2 us (4%)
    another operation x16, other arithmetic, deluxe_solve(): factor = jnp.linalg.cholesky(summed_matrix)  322 us
    another operation x5, other arithmetic, deluxe_solve(): lax.linalg.triangular_solve(factor, inner_part, left_side=True, lower=Tru...  166 us
    dot_general x1, matrix products, condense(): jnp.dot(couple.reshape(face_count * face_size, inner_size), inverse, prec...  32.7 us
    ppermute x6, waiting for transfers between devices, from_behind(): return lax.ppermute(block, axis, route)  22.9 us
    ppermute x2, waiting for transfers between devices, padded(): after = lax.ppermute(first, axis, down)  18.8 us
    dot_general x1, matrix products, condense(): jnp.einsum('fan,fbn->fab', left_part, couple, precision=lax.Precision.HIG...  16.4 us
    another operation x6, matrix products, deluxe_solve(): factor = jnp.linalg.cholesky(summed_matrix)  15.9 us
    another operation x12, local copies, waits for them, and re-layouts  15.3 us
  transfers between devices with their start and end apart: 10, of which 10 were waited for; matrix products, arithmetic and copies ran while one was open for 0% of the time, Pallas kernels for 0%

commit v1 on v0

v1 whole, which is shorter than its diff:
```python
import functools

import jax
import jax.numpy as jnp
from jax import lax
from jax.experimental import pallas as pl
from jax.experimental.pallas import tpu as pltpu
from jax.sharding import PartitionSpec as P

CB = 128
TILE = 256
NB = 128
GROUP = 2
F32 = jnp.float32
BF16 = jnp.bfloat16
NN = (((1,), (0,)), ((), ()))
NT = (((1,), (1,)), ((), ()))
MESH = pl.DeviceIdType.MESH
ANY = pl.BlockSpec(memory_space=pl.ANY)
WHOLE = pl.BlockSpec(memory_space=pltpu.VMEM)
SCALARS = pl.BlockSpec(memory_space=pltpu.SMEM)


def halves(x):
    hi = x.astype(BF16)
    lo = (x - hi.astype(F32)).astype(BF16)
    return hi, lo


def mul(a, b, dims=NN):
    return lax.dot_general(a, b, dims, preferred_element_type=F32)


def dot3(a, b, dims=NN):
    ah, al = a if isinstance(a, tuple) else halves(a)
    bh, bl = b if isinstance(b, tuple) else halves(b)
    return mul(ah, bh, dims) + (mul(ah, bl, dims) + mul(al, bh, dims))


def place():
    ix, iy = lax.axis_index("gx"), lax.axis_index("gy")
    nx, ny = lax.axis_size("gx"), lax.axis_size("gy")

    def at(dx, dy):
        return (lax.rem(ix + dx + nx, nx), lax.rem(iy + dy + ny, ny))

    return ix, iy, nx, ny, at


def greet(devices):
    barrier = pltpu.get_barrier_semaphore()
    for device in devices:
        pl.semaphore_signal(barrier, inc=1, device_id=device, device_id_type=MESH)
    pl.semaphore_wait(barrier, len(devices))


def remote(src, dst, send_sem, recv_sem, device):
    return pltpu.make_async_remote_copy(
        src_ref=src, dst_ref=dst, send_sem=send_sem, recv_sem=recv_sem, device_id=device, device_id_type=MESH
    )


def schur_into(out_ref, a_ref, c_hi, c_lo, t_hi, t_lo, acc):
    width = c_hi.shape[1]
    for j in range(width // TILE):
        cols = slice(j * TILE, (j + 1) * TILE)
        rest = slice(j * TILE, width)
        w = dot3((c_hi[:, rest], c_lo[:, rest]), (t_hi[rest, cols], t_lo[rest, cols]))
        part = dot3(w, (c_hi[:, cols], c_lo[:, cols]), NT)
        if j == 0:
            acc[...] = part
        else:
            acc[...] += part
    x = acc[...]
    out_ref[...] = a_ref[...] - (x + x.T)


def schur_kernel(
    c_any, k_any, a_any, v_ref,
    m_ref, rhs_ref, nb_ref,
    k_ref, c_ref, a_ref, t_hi, t_lo, c_hi, c_lo, acc, s_ref, r_ref,
    k_sem, c_sem, a_sem, vs_sem, vr_sem, ss_sem, sr_sem,
):
    ix, iy, nx, ny, at = place()
    odd = lax.rem(ix, 2)
    step = 2 * odd - 1
    to = (at(0, step), at(-1, 0))
    size, width = c_hi.shape
    tiles = width // TILE
    half = size // 2
    faces = (2 + odd, 0, 3 - odd, 1)

    def k_copy(i):
        rows, cols = pl.ds(i * TILE, TILE), pl.ds(0, (i + 1) * TILE)
        return pltpu.make_async_copy(k_any.at[0, 0, rows, cols], k_ref.at[rows, cols], k_sem.at[i])

    def c_copy(s):
        return pltpu.make_async_copy(c_any.at[0, 0, faces[s]], c_ref.at[s % 2], c_sem.at[s % 2])

    def a_copy(s):
        return pltpu.make_async_copy(a_any.at[0, 0, faces[s]], a_ref.at[s % 2], a_sem.at[s % 2])

    c_copy(0).start()
    for i in reversed(range(tiles)):
        k_copy(i).start()
    a_copy(0).start()
    c_copy(1).start()
    a_copy(1).start()
    greet((at(0, 1), at(0, -1), at(1, 0), at(-1, 0)))
    v_copies = [remote(v_ref.at[0, 0, faces[s]], nb_ref.at[s], vs_sem.at[s], vr_sem.at[s], to[s]) for s in range(2)]
    for copy in v_copies:
        copy.start()

    parts = ((pl.ds(half, half), pl.ds(0, size)), (pl.ds(0, half), pl.ds(0, half)))
    s_copies = [
        [remote(s_ref.at[(s, *part)], r_ref.at[(s, *part)], ss_sem.at[s, n], sr_sem.at[s, n], to[s]) for n, part in enumerate(parts)]
        for s in range(2)
    ]
    c_copy(0).wait()
    c_hi[...], c_lo[...] = halves(c_ref[0])
    for i in reversed(range(tiles)):
        k_copy(i).wait()
        for j in range(i + 1):
            rows, cols = slice(i * TILE, (i + 1) * TILE), slice(j * TILE, (j + 1) * TILE)
            t = k_ref[rows, cols]
            t_hi[rows, cols], t_lo[rows, cols] = halves(0.5 * t if i == j else t)
    for s in range(4):
        if s > 0:
            c_copy(s).wait()
            c_hi[...], c_lo[...] = halves(c_ref[s % 2])
        a_copy(s).wait()
        out = s_ref.at[s] if s < 2 else m_ref.at[s - 2]
        schur_into(out, a_ref.at[s % 2], c_hi, c_lo, t_hi, t_lo, acc)
        if s < 2:
            c_copy(s + 2).start()
            a_copy(s + 2).start()
            for copy in s_copies[s]:
                copy.start()
        else:
            f = s - 2
            v_copies[f].wait()
            rhs_ref[f] = dot3(m_ref[f], v_ref[0, 0, faces[s]] - nb_ref[f])
    for f in range(2):
        for copy in s_copies[f]:
            copy.wait()
        m_ref[f, :half, :half] += r_ref[f, :half, :half]
        low = r_ref[f, half:, :]
        m_ref[f, half:, :] += low
        m_ref[f, :half, half:] += low[:, :half].T


def schur_call(couple, inverse, blocks, values):
    size, width = couple.shape[3:]
    rhs = values.shape[4]
    dma = pltpu.SemaphoreType.DMA
    return pl.pallas_call(
        schur_kernel,
        in_specs=[ANY, ANY, ANY, WHOLE],
        out_specs=[WHOLE] * 3,
        out_shape=[
            jax.ShapeDtypeStruct((2, size, size), F32),
            jax.ShapeDtypeStruct((2, size, rhs), F32),
            jax.ShapeDtypeStruct((2, size, rhs), F32),
        ],
        scratch_shapes=[
            pltpu.VMEM((width, width), F32),
            pltpu.VMEM((2, size, width), F32),
            pltpu.VMEM((2, size, size), F32),
            pltpu.VMEM((width, width), BF16),
            pltpu.VMEM((width, width), BF16),
            pltpu.VMEM((size, width), BF16),
            pltpu.VMEM((size, width), BF16),
            pltpu.VMEM((size, size), F32),
            pltpu.VMEM((2, size, size), F32),
            pltpu.VMEM((2, size, size), F32),
            dma((width // TILE,)), dma((2,)), dma((2,)), dma((2,)), dma((2,)), dma((2, 2)), dma((2, 2)),
        ],
        compiler_params=pltpu.CompilerParams(collective_id=1, has_side_effects=True),
        name="schur",
    )(couple, inverse, blocks, values)


def lane(x, k):
    return jnp.broadcast_to(x[:, :, k : k + 1], x.shape)


def sub(x, k):
    return jnp.broadcast_to(x[:, k : k + 1, :], x.shape)


def stacked(left):
    return jnp.concatenate(halves(left), axis=1)


def doubled(hi, lo):
    return jnp.concatenate(
        [jnp.concatenate([hi, lo], axis=1), jnp.concatenate([hi, jnp.zeros_like(lo)], axis=1)], axis=0
    )


def prod3(left, right):
    out = mul(stacked(left), doubled(*halves(right)), NN)
    n = right.shape[1]
    return out[:, :n] + out[:, n:]


def eliminate_panel(tiles, p, base, rows, cols):
    start = 8 * (base + p)
    span = (cols >= start) & (cols < start + 8)
    others = [q for q in range(p + 1, len(tiles))] + [q for q in range(p)]
    c = [lane(tiles[p], start + j) for j in range(8)]
    g = {q: [lane(tiles[q], start + j) for j in range(8)] for q in others}
    u = jnp.where(span, jnp.where(cols - start == rows, 1.0, 0.0), tiles[p])
    for j in range(8):
        r = sub(1.0 / c[j], j)
        f = jnp.where(rows == j, 1.0 - r, c[j] * r)
        for m in range(j + 1, 8):
            c[m] = c[m] - f * sub(c[m], j)
        u = u - f * sub(u, j)
    u_rows = [sub(u, j) for j in range(8)]
    for q in others:
        terms = [g[q][j] * u_rows[j] for j in range(8)]
        while len(terms) > 1:
            terms = [terms[i] + terms[i + 1] for i in range(0, len(terms), 2)]
        tiles[q] = jnp.where(span, 0.0, tiles[q]) - terms[0]
    tiles[p] = u


def invert(tiles, side_work):
    faces, _, n = tiles[0].shape
    shape = tiles[0].shape
    rows = lax.broadcasted_iota(jnp.int32, shape, 1)
    cols = lax.broadcasted_iota(jnp.int32, shape, 2)
    count = len(tiles)
    for base in range(0, count, GROUP):
        mine = tiles[base : base + GROUP]
        rest = [q for q in range(count) if not base <= q < base + GROUP]
        left = [stacked(jnp.concatenate([tiles[q][f] for q in rest], axis=0)) for f in range(faces)]
        for p in range(GROUP):
            eliminate_panel(mine, p, base, rows, cols)
            if side_work:
                side_work.pop(0)()
        span = (cols >= 8 * base) & (cols < 8 * (base + GROUP))
        out = []
        for f in range(faces):
            v = jnp.concatenate([m[f] for m in mine], axis=0)
            hi, lo = halves(v)
            wide = jnp.concatenate([jnp.concatenate([hi, lo], axis=1), jnp.concatenate([hi, jnp.zeros_like(lo)], axis=1)], axis=0)
            zero = lambda m: jnp.zeros((m, 2 * n), BF16)
            top, low = 8 * base, n - 8 * (base + GROUP)
            one = lambda part: [zero(top)] * (top > 0) + [part] + [zero(low)] * (low > 0)
            half = 8 * GROUP
            right = jnp.concatenate(one(wide[:half]) + one(wide[half:]), axis=0)
            o = mul(left[f], right, NN)
            out.append(o[:, :n] + o[:, n:])
        for i, q in enumerate(rest):
            upd = jnp.stack([out[f][8 * i : 8 * i + 8] for f in range(faces)])
            tiles[q] = jnp.where(span, 0.0, tiles[q]) - upd
        tiles[base : base + GROUP] = mine
    while side_work:
        side_work.pop(0)()


def solve_kernel(s_ref, rhs_ref, nb_ref, x_ref, m_ref, hi_ref, lo_ref):
    faces, size, width = rhs_ref.shape
    count = size // NB
    total = size + width
    m_ref[:, :, :size] = s_ref[...]
    m_ref[:, :, size:] = rhs_ref[...]
    side_work = []
    for k in range(count):
        rk = slice(k * NB, (k + 1) * NB)
        tiles = [m_ref[:, k * NB + 8 * q : k * NB + 8 * q + 8, rk] for q in range(NB // 8)]
        invert(tiles, side_work)
        inv = [stacked(jnp.concatenate([t[f] for t in tiles], axis=0)) for f in range(faces)]

        def scale(f, cols, inv=inv, rk=rk):
            hi, lo = halves(m_ref[f, rk, cols])
            out = mul(inv[f], jnp.concatenate([hi, hi], axis=0), NN) + mul(inv[f][:, :NB], lo, NN)
            m_ref[f, rk, cols] = out
            hi_ref[f, :, cols], lo_ref[f, :, cols] = halves(out)

        def update(f, i, cols, rk=rk):
            ri = slice(i * NB, (i + 1) * NB)
            left = stacked(m_ref[f, ri, rk])
            hi = hi_ref[f, :, cols]
            m_ref[f, ri, cols] -= mul(left, jnp.concatenate([hi, hi], axis=0), NN) + mul(
                left[:, :NB], lo_ref[f, :, cols], NN
            )

        if k < count - 1:
            near = slice((k + 1) * NB, (k + 2) * NB)
            far = slice((k + 2) * NB, total)
            for f in range(faces):
                scale(f, near)
            for f in range(faces):
                update(f, k + 1, near)
            side_work += [functools.partial(scale, f, far) for f in range(faces)]
            side_work += [functools.partial(update, f, k + 1, far) for f in range(faces)]
            for i in range(count):
                if i not in (k, k + 1):
                    side_work += [functools.partial(update, f, i, slice((k + 1) * NB, total)) for f in range(faces)]
        else:
            for f in range(faces):
                scale(f, slice(size, total))
                for i in range(count - 1):
                    update(f, i, slice(size, total))
    for f in range(faces):
        x_ref[f] = nb_ref[f] + m_ref[f, :, size:]


def solve_call(m, rhs, nb):
    _, size, width = rhs.shape
    return pl.pallas_call(
        solve_kernel,
        in_specs=[WHOLE] * 3,
        out_specs=WHOLE,
        out_shape=jax.ShapeDtypeStruct((2, size, width), F32),
        scratch_shapes=[
            pltpu.VMEM((2, size, size + width), F32),
            pltpu.VMEM((2, NB, size + width), BF16),
            pltpu.VMEM((2, NB, size + width), BF16),
        ],
        name="solve",
    )(m, rhs, nb)


def coarse_kernel(
    count_ref, adj_ref, map_ref, x_ref, v_ref, basis_any, matrix_any,
    avg_any, out_ref,
    avg, basis, matrix, ret, outgoing, incoming,
    b_sem, m_sem, o_sem, rs_sem, rr_sem, s_sem, r_sem,
):
    ix, iy, nx, ny, at = place()
    odd = lax.rem(ix, 2)
    step = 2 * odd - 1
    size, rhs = x_ref.shape[1:]
    primal = matrix.shape[0]
    b_copy = pltpu.make_async_copy(basis_any.at[0, 0], basis, b_sem)
    m_copy = pltpu.make_async_copy(matrix_any.at[0, 0], matrix, m_sem)
    b_copy.start()
    m_copy.start()
    down = (at(0, -1), at(-1, 0), at(-1, -1))
    up = (at(0, 1), at(1, 0), at(1, 1))
    greet(down + up)
    back = (at(0, -step), at(1, 0))
    returns = [remote(x_ref.at[f], ret.at[f], rs_sem.at[f], rr_sem.at[f], back[f]) for f in range(2)]
    for copy in returns:
        copy.start()

    own, other = 3 - odd, 2 + odd

    def out_copy(face, n):
        return pltpu.make_async_copy(avg.at[face], avg_any.at[0, 0, face], o_sem.at[n])

    def glued(f, face, new):
        avg[face] = jnp.where(adj_ref[0, 0, face] > 0, new, v_ref[0, 0, face])
        out_copy(face, f).start()

    glued(0, own, x_ref[0])
    glued(1, 1, x_ref[1])
    rows = map_ref[0]
    window = ((ix - (rows >> 11)) * 2 + iy - ((rows >> 7) & 15)) * CB + (rows & 127)
    live = lax.broadcasted_iota(jnp.int32, rows.shape, 1) < count_ref[0, 0]
    window = jnp.where(live, window, -1)
    spots = lax.broadcasted_iota(jnp.int32, (4 * CB, primal), 0)
    hot = jnp.where(spots == window, 1.0, 0.0).astype(BF16)
    b_copy.wait()

    def part(face):
        start = face * size
        if not isinstance(face, int):
            start = pl.multiple_of(start, size)
        return dot3(avg[face].T, basis[pl.ds(start, size), :])

    total = part(own) + part(1)
    m_copy.wait()
    mh, ml = halves(matrix[...])
    for copy in returns:
        copy.wait()
    glued(2, other, ret[0])
    glued(3, 0, ret[1])
    total += part(other) + part(0)

    def spread(x):
        hi, lo = halves(x)
        return mul(hi, hot, NT) + mul(lo, hot, NT)

    def blocks(n, devices, arrays):
        copies = []
        for b in range(3):
            outgoing[n, b] = arrays[b]
            copies.append(remote(outgoing.at[n, b], incoming.at[n, b], s_sem.at[n, b], r_sem.at[n, b], devices[b]))
            copies[b].start()
        return copies

    inside_x, inside_y = ix < nx - 1, iy < ny - 1

    def assemble(n, terms):
        copies = blocks(n, down, [terms[:, b * CB : (b + 1) * CB] for b in range(1, 4)])
        for copy in copies:
            copy.wait()
        return (
            terms[:, :CB]
            + jnp.where(inside_y, incoming[n, 0], 0.0)
            + jnp.where(inside_x, incoming[n, 1], 0.0)
            + jnp.where(jnp.logical_and(inside_x, inside_y), incoming[n, 2], 0.0)
        )

    residual = assemble(0, spread(total))
    copies = blocks(1, up, [residual] * 3)
    for copy in copies:
        copy.wait()
    wide = jnp.concatenate([residual, incoming[1, 0], incoming[1, 1], incoming[1, 2]], axis=1)
    hi, lo = halves(wide)
    picked = mul(hi, hot) + mul(lo, hot)
    local = dot3(picked, (mh, ml), NT)
    out_ref[...] = assemble(2, spread(local)).T
    for n, face in enumerate((own, 1, other, 0)):
        out_copy(face, n).wait()


def coarse_call(count, adjacency, rows, x, values, basis, matrix):
    size, rhs = x.shape[1:]
    primal = matrix.shape[2]
    dma = pltpu.SemaphoreType.DMA
    return pl.pallas_call(
        coarse_kernel,
        in_specs=[SCALARS, SCALARS, WHOLE, WHOLE, WHOLE, ANY, ANY],
        out_specs=[ANY, WHOLE],
        out_shape=[jax.ShapeDtypeStruct(values.shape, F32), jax.ShapeDtypeStruct((CB, rhs), F32)],
        scratch_shapes=[
            pltpu.VMEM(values.shape[2:], F32),
            pltpu.VMEM(basis.shape[2:], F32),
            pltpu.VMEM((primal, primal), F32),
            pltpu.VMEM((2, size, rhs), F32),
            pltpu.VMEM((3, 3, rhs, CB), F32),
            pltpu.VMEM((3, 3, rhs, CB), F32),
            dma, dma, dma((4,)), dma((2,)), dma((2,)), dma((3, 3)), dma((3, 3)),
        ],
        compiler_params=pltpu.CompilerParams(collective_id=2, has_side_effects=True),
        name="coarse",
    )(count, adjacency, rows, x, values, basis, matrix)


def shards(
    face_block,
    coupling,
    interior_inverse,
    face_values,
    adjacency,
    primal_basis,
    primal_matrix,
    primal_map,
    primal_count,
):
    m, rhs, nb = schur_call(coupling, interior_inverse, face_block, face_values)
    x = solve_call(m, rhs, nb)
    return coarse_call(primal_count, adjacency, primal_map, x, face_values, primal_basis, primal_matrix)


def solution(mesh):
    in_specs = (
        P("gx", "gy", None, None, None),
        P("gx", "gy", None, None, None),
        P("gx", "gy", None, None),
        P("gx", "gy", None, None, None),
        P("gx", "gy", None),
        P("gx", "gy", None, None),
        P("gx", "gy", None, None),
        P("gx", "gy", None),
        P("gx", "gy"),
    )
    out_specs = (P("gx", "gy", None, None, None), P(("gx", "gy"), None))
    return jax.shard_map(shards, mesh=mesh, in_specs=in_specs, out_specs=out_specs, check_vma=False)
```

time: 723 us -> 96.5 us (0.13); the launches traced: 710 us -> 96.2 us
  other arithmetic: 508 us -> 0 us
  Pallas kernels: 0 us -> 91.1 us
  matrix products: 88.9 us -> 0 us
  waiting for transfers between devices: 47.8 us -> 0 us
  local copies, waits for them, and re-layouts: 37.6 us -> 3.74 us
  starting transfers between devices: 26.2 us -> 0 us
    another operation x23 -> x0, other arithmetic: 488 us -> none  [the longest x16 322 us: deluxe_solve(): factor = jnp.linalg.cholesky(summed_matrix)]
    pallas_call x0 -> x3, Pallas kernels: none -> 91.1 us  [the longest x1 38.5 us: schur_call(): pl.pallas_call(schur_kernel, in_specs=[ANY, ANY, ANY, WHOLE], out_specs=[...]
    dot_general x5 -> x0, matrix products: 56.8 us -> none  [the longest x1 32.7 us: condense(): jnp.dot(couple.reshape(face_count * face_size, inner_size), inverse, prec...]
    ppermute x10 -> x0, waiting for transfers between devices: 47.8 us -> none  [the longest x6 22.9 us: from_behind(): return lax.ppermute(block, axis, route)]
    another operation x20 -> x0, matrix products: 32.2 us -> none  [the longest x6 15.9 us: deluxe_solve(): factor = jnp.linalg.cholesky(summed_matrix)]
    ppermute x10 -> x0, starting transfers between devices: 26.2 us -> none  [the longest x6 12.9 us: from_behind(): return lax.ppermute(block, axis, route)]
    another operation x18 -> x0, local copies, waits for them, and re-layouts: 20 us -> none
  transfers between devices with their start and end apart: 10 -> 0, of which waited for: 10 -> 0; matrix products, arithmetic and copies ran while one was open for 0% -> 0% of each run, Pallas kernels for 0% -> 0%
where the time goes in v1:
time: 96.5 us; the launch traced here: 96.2 us
  Pallas kernels  91.1 us (94%)
  local copies, waits for them, and re-layouts  3.74 us (4%)
  between operations  1.3 us (1%)
    pallas_call x1, Pallas kernels, schur_call(): pl.pallas_call(schur_kernel, in_specs=[ANY, ANY, ANY, WHOLE], out_specs=[...  38.5 us
    pallas_call x1, Pallas kernels, coarse_call(): pl.pallas_call(coarse_kernel, in_specs=[SCALARS, SCALARS, WHOLE, WHOLE, W...  30.2 us
    pallas_call x1, Pallas kernels, solve_call(): pl.pallas_call(solve_kernel, in_specs=[WHOLE] * 3, out_specs=WHOLE, out_s...  22.4 us
    unnamed x2, local copies, waits for them, and re-layouts  3.74 us

profile of v1, /device:TPU:1, one launch (start us, length us, event | category | flops | bytes accessed | tf_op | source)
XLA Modules:
  0.0 96.2 jit_solution(13543267763417084433)
XLA Ops:
  0.6 38.5 %schur.1 = (f32[2,512,512]{2,1,0:T(8,128)}, f32[2,512,128]{2,1,0:T(8,128)}, f32[2,512,128]{2,1,0:T(8,128)}) custom-call(f32[1,1,4,512,1024]{4,3,2,1,0:T(8,128)} %c_any.1, f32[1,1,1024,1024]{3,2,1,0:T(8,128)} %k_any.1, f32[1,1,4,512,512]{4,3,2,1,0:T(8,128)} %a_any.1, f32[1,1,4,512,128]{4,3,2,1,0:T(8,128)} %v_ref.3), custom_call_target="tpu_custom_call" | custom-call | tf_op jit(solution)/shard_map/schur/pallas_call | solution.py:156
  39.1 22.4 %solve.1.x_ref = f32[2,512,128]{2,1,0:T(8,128)} custom-call(f32[2,512,512]{2,1,0:T(8,128)} %get-tuple-element.5.s_ref, f32[2,512,128]{2,1,0:T(8,128)} %get-tuple-element.6.rhs_ref, f32[2,512,128]{2,1,0:T(8,128)} %get-tuple-element.7.nb_ref), custom_call_target="tpu_custom_call" | custom-call | tf_op jit(solution)/shard_map/solve/pallas_call | solution.py:314
  62.2 30.2 %coarse.1 = (f32[1,1,4,512,128]{4,3,2,1,0:T(8,128)}, f32[128,128]{1,0:T(8,128)}) custom-call(s32[1,1]{1,0:T(1,128)S(6)} %copy.13.count_ref, s32[1,1,4]{2,1,0:T(1,128)} %adj_ref.1, s32[1,1,384]{2,1,0:T(1,128)} %map_ref.1, f32[2,512,128]{2,1,0:T(8,128)} %solve.1.x_ref, f32[1,1,4,512,128]{4,3,2,1,0:T(8,128)} %v_ref.3, f32[1,1,2048,384]{3,2,1,0:T(8,128)} %basis_any.1, ...), custom_call_target="tpu_custom_call" | custom-call | tf_op jit(solution)/shard_map/coarse/pallas_call | solution.py:427
  92.4 2.3 %copy.14 = f32[1,1,4,512,128]{4,3,2,1,0:T(8,128)} copy(f32[1,1,4,512,128]{4,3,2,1,0:T(8,128)} %get-tuple-element.10) | data formatting | bytes 2097152
  94.7 1.5 %copy.15 = f32[128,128]{1,0:T(8,128)} copy(f32[128,128]{1,0:T(8,128)} %get-tuple-element.11) | data formatting | bytes 131072
